TPU v7x, 128 devices: a whole 4x4x4 slice. The times are simulated.
128 devices in a mesh: rep: 8 (over y_hi, z), fsdp: 16 (over y_lo, x, core).
Axes of the slice: x: 4, y: 4 (y_hi: 2, y_lo: 2; y = y_hi * 2 + y_lo), z: 4, core: 2. Of those that a mesh axis runs over, the one named last changes fastest.
Arguments:
- attn_out: bfloat16 [8, 4096, 2560], P('rep', 'fsdp'), may hold values from -6 to 6
- residual: bfloat16 [8, 4096, 5120], P('rep', 'fsdp'), may hold values from -400 to 400
- cotangent: bfloat16 [8, 4096, 5120], P('rep', 'fsdp'), may hold values from -2 to 2
- norm_gain: bfloat16 [5120], P('fsdp'), may hold values from 0.29882812 to 3
- params: float32 [8, 5120, 2560], P('rep', 'fsdp'), may hold values from -1 to 1
- first_moment: float32 [8, 5120, 2560], P('rep', 'fsdp'), may hold values from -3 to 3
- second_moment: float32 [8, 5120, 2560], P('rep', 'fsdp'), may hold values from 0.05 to 2
- step_count: int32 [1], replicated, may hold values from 0 to 63
Outputs:
- params_out: float32 [8, 5120, 2560], P('rep', 'fsdp')
- first_out: float32 [8, 5120, 2560], P('rep', 'fsdp')
- second_out: float32 [8, 5120, 2560], P('rep', 'fsdp')
All inputs are finite; a program needn't handle non-finite values.
Results may differ from a plain program's by a relative error of at most 0.007.
Values may be sent and summed in bfloat16 or wider, within the bound.
A program may use at most 192 MiB of HBM per device.

v0:
```python
from functools import partial
import jax
import jax.numpy as jnp
from jax import lax
from jax.sharding import PartitionSpec as P

beta_one = 0.9
beta_two = 0.999
learn_rate = 0.001
decay_rate = 0.1
norm_eps = 1e-05
adam_eps = 1e-08


def partner(value, axis, bit):
    mask = 2**bit
    pairs = [(source, source ^ mask) for source in range(lax.axis_size(axis))]
    return lax.ppermute(value, axis, pairs)


def norm_backward(pre_norm, scaled, square_sum, cross_sum, width_total):
    inv_rms = lax.rsqrt(square_sum / width_total + norm_eps)
    correction = inv_rms * inv_rms * inv_rms * cross_sum / width_total
    return (inv_rms[:, None] * scaled - pre_norm * correction[:, None]).astype(jnp.bfloat16)


def adam_change(params_local, gradient, first_local, second_local, step_count):
    step_time = (step_count[0] + 1).astype(jnp.float32)
    first_fix = 1.0 - jnp.power(jnp.float32(beta_one), step_time)
    second_fix = 1.0 - jnp.power(jnp.float32(beta_two), step_time)
    first_new = beta_one * first_local + (1.0 - beta_one) * gradient
    second_new = beta_two * second_local + (1.0 - beta_two) * gradient * gradient
    update_step = -learn_rate * (
        first_new / first_fix / (jnp.sqrt(second_new / second_fix) + adam_eps)
        + decay_rate * params_local
    )
    return (update_step, first_new, second_new)


def swap_updated(shard_data, bit_number):
    return partner(shard_data, "rep", bit_number)


def pick_partner(shard_data, partner_level, helper, level_count):
    branches = [partial(helper, bit_number=number) for number in range(level_count)]
    return lax.switch(partner_level, branches, shard_data)


def per_device(
    attn_out, residual, cotangent, norm_gain, params, first_moment, second_moment, step_count
):
    local_attn = attn_out[0]
    width_total = residual.shape[2]
    params_local = params[0]
    w_half = params_local.astype(jnp.bfloat16)
    contract_feat = (((1,), (1,)), ((), ()))
    contract_rows = (((0,), (0,)), ((), ()))
    full_attn = lax.all_gather(local_attn, "fsdp", axis=0, tiled=True)
    pre_cols = lax.dot_general(full_attn, w_half, contract_feat, preferred_element_type=jnp.float32)
    resid_cols, cotan_cols = (
        lax.all_to_all(residual[0], "fsdp", split_axis=1, concat_axis=0, tiled=True),
        lax.all_to_all(cotangent[0], "fsdp", split_axis=1, concat_axis=0, tiled=True),
    )
    pre_norm = resid_cols.astype(jnp.float32) + pre_cols
    scaled = norm_gain.astype(jnp.float32)[None, :] * cotan_cols.astype(jnp.float32)
    square_sum, cross_sum = (
        lax.psum(jnp.sum(pre_norm * pre_norm, axis=1).astype(jnp.bfloat16), "fsdp").astype(
            jnp.float32
        ),
        lax.psum(jnp.sum(pre_norm * scaled, axis=1).astype(jnp.bfloat16), "fsdp").astype(
            jnp.float32
        ),
    )
    grad_pre = norm_backward(pre_norm, scaled, square_sum, cross_sum, width_total)
    gradient = lax.dot_general(
        grad_pre, full_attn, contract_rows, preferred_element_type=jnp.float32
    )
    update_step, first_new, second_new = adam_change(
        params_local, gradient, first_moment[0], second_moment[0], step_count
    )
    level_count = lax.axis_size("rep").bit_length() - 1
    partner_level = jnp.remainder(step_count[0], level_count)
    updated = params_local + update_step
    updated_far = pick_partner(updated, partner_level, swap_updated, level_count)
    params_change = 0.5 * (updated_far - params_local) + 0.5 * update_step
    return (params_change[None], first_new[None], second_new[None])


def solution(mesh):
    return jax.shard_map(
        per_device,
        mesh=mesh,
        in_specs=(
            P("rep", "fsdp", None),
            P("rep", "fsdp", None),
            P("rep", "fsdp", None),
            P("fsdp"),
            P("rep", "fsdp", None),
            P("rep", "fsdp", None),
            P("rep", "fsdp", None),
            P(),
        ),
        out_specs=(P("rep", "fsdp", None), P("rep", "fsdp", None), P("rep", "fsdp", None)),
        check_vma=False,
    )
```

profile of v0, /device:TPU:0, one launch (start us, length us, event | category | flops | bytes accessed | tf_op | source)
XLA Modules:
  0.0 361.3 jit_solution(13053667947359435022)
XLA Ops:
  7.2 0.0 all-gather.3.cloned.1.call-start
  7.2 0.7 all-gather.3.cloned.1.call-update
  7.9 4.4 %copy.13 = bf16[1,256,5120]{1,2,0:T(8,128)(2,1)} copy(bf16[1,256,5120]{2,1,0:T(8,128)(2,1)} %param.12) | data formatting | bytes 5242880 | tf_op args[1]
  12.3 5.5 %all-to-all-start = ((bf16[256,16,320]{0,2,1:T(8,128)(2,1)}), bf16[256,16,320]{0,2,1:T(8,128)(2,1)S(1)}, u32[]{:S(2)}, u32[]{:S(2)}) async-start(bf16[256,16,320]{0,2,1:T(8,128)(2,1)} %bitcast.3), calls=%async_computation | async-start | bytes 5242880 | tf_op jit(solution)/shard_map/all_to_all | solution.py:61
  17.8 4.4 %copy.15 = bf16[1,256,5120]{1,2,0:T(8,128)(2,1)} copy(bf16[1,256,5120]{2,1,0:T(8,128)(2,1)} %param.13) | data formatting | bytes 5242880 | tf_op args[2]
  22.2 0.0 copy-start.1
  22.2 51.5 %all-to-all-done = bf16[256,16,320]{0,2,1:T(8,128)(2,1)S(1)} async-done(((bf16[256,16,320]{0,2,1:T(8,128)(2,1)}), bf16[256,16,320]{0,2,1:T(8,128)(2,1)S(1)}, u32[]{:S(2)}, u32[]{:S(2)}) %all-to-all-start) | async-done | bytes 2621472 | tf_op jit(solution)/shard_map/all_to_all | solution.py:61
  73.7 6.6 %all-to-all-start.1 = ((bf16[256,16,320]{0,2,1:T(8,128)(2,1)}), bf16[256,16,320]{0,2,1:T(8,128)(2,1)}, u32[]{:S(2)}, u32[]{:S(2)}) async-start(bf16[256,16,320]{0,2,1:T(8,128)(2,1)} %bitcast.6), calls=%async_computation.1 | async-start | bytes 5242880 | tf_op jit(solution)/shard_map/all_to_all | solution.py:62
  81.0 0.0 copy-done.1
  81.1 0.6 convert_bitcast_fusion.1
  81.6 3.0 copy.17
  84.6 55.3 %all-to-all-done.1 = bf16[256,16,320]{0,2,1:T(8,128)(2,1)} async-done(((bf16[256,16,320]{0,2,1:T(8,128)(2,1)}), bf16[256,16,320]{0,2,1:T(8,128)(2,1)}, u32[]{:S(2)}, u32[]{:S(2)}) %all-to-all-start.1) | async-done | bytes 2621472 | tf_op jit(solution)/shard_map/all_to_all | solution.py:62
  139.9 2.3 convert_bitcast_fusion
  142.3 0.0 copy-start
  142.3 3.0 copy.18
  145.2 32.3 %all-gather.3.cloned.1.call-done = bf16[1,4096,2560]{2,1,0:T(8,128)(2,1)} async-done(((bf16[1,256,2560]{2,1,0:T(8,128)(2,1)}), bf16[1,4096,2560]{2,1,0:T(8,128)(2,1)}) %all-gather.3.cloned.1.call-update) | async-done | bytes 20971536 | tf_op jit(solution)/shard_map/all_gather | solution.py:58
  177.5 0.0 copy-done
  177.5 24.1 %multiply_reduce_fusion.1 = (bf16[4096]{0:T(1024)(128)(2,1)S(1)}, bf16[4096]{0:T(1024)(128)(2,1)S(1)}, f32[4096,320]{0,1:T(8,128)}) fusion(f32[4096,320]{0,1:T(8,128)} %bitcast.77, f32[320]{0:T(512)S(1)} %convert_element_type.49, f32[4096,320]{0,1:T(8,128)} %bitcast.79, bf16[1,4096,2560]{2,1,0:T(8,128)(2,1)} %all-gather.3.cloned.1.call-done, ...), kind=kOutput, calls=%fused_computation.9 | convolution fusion | flops 6718742528 | bytes 39994624 | tf_op jit(solution)/shard_map/dot_general | solution.py:59
  201.6 55.2 %all-reduce = (bf16[4096]{0:T(1024)(128)(2,1)S(1)}, bf16[4096]{0:T(1024)(128)(2,1)S(1)}) all-reduce(bf16[4096]{0:T(1024)(128)(2,1)S(1)} %get-tuple-element.11, bf16[4096]{0:T(1024)(128)(2,1)S(1)} %get-tuple-element.10), channel_id=1, replica_groups=mesh['rep'=8,'fsdp'=16] {'fsdp'}, use_global_device_ids=true, to_apply=%region_3.0 | all-reduce | flops 8192 | bytes 32768 | tf_op jit(solution)/shard_map/psum | solution.py:70
  256.9 19.5 %bitcast_add_fusion.1 = (f32[320,2560]{1,0:T(8,128)}, f32[320,2560]{1,0:T(8,128)}) fusion(f32[1,320,2560]{2,1,0:T(8,128)S(1)} %copy-done, f32[]{:T(128)} %bitcast.10, f32[1,320,2560]{2,1,0:T(8,128)} %param.17, f32[]{:T(128)} %bitcast.8, f32[1,320,2560]{2,1,0:T(8,128)} %param.16, bf16[1,4096,2560]{2,1,0:T(8,128)(2,1)} %all-gather.3.cloned.1.call-done, ...), kind=kOutput, calls=%fused_computation.14 | convolution fusion | flops 6729728000 | bytes 47875336 | tf_op jit(solution)/shard_map/dot_general | solution.py:75
  276.4 69.4 %conditional.1 = (f32[320,2560]{1,0:T(8,128)}) conditional(s32[]{:T(128)} %clamp.3, f32[320,2560]{1,0:T(8,128)} %get-tuple-element.20, f32[320,2560]{1,0:T(8,128)} %get-tuple-element.20, f32[320,2560]{1,0:T(8,128)} %get-tuple-element.20), branch_computations={%region_4.5_spmd, %region_5.6_spmd, %region_6.7_spmd} | conditional | bytes 13107248 | solution.py:46
  276.4 1.9 collective-permute-start
  278.3 67.5 %collective-permute-done = f32[320,2560]{1,0:T(8,128)} collective-permute-done((f32[320,2560]{1,0:T(8,128)}, f32[320,2560]{1,0:T(8,128)}, u32[]{:S(2)}, u32[]{:S(2)}) %collective-permute-start) | collective-permute-done | bytes 3276832 | tf_op jit(solution)/shard_map/cond/branch_0_fun/ppermute | solution.py:18
  345.8 8.7 %fusion.16 = (f32[1,320,2560]{2,1,0:T(8,128)}, f32[1,320,2560]{2,1,0:T(8,128)}, f32[1,320,2560]{2,1,0:T(8,128)}) fusion(f32[320,2560]{1,0:T(8,128)} %get-tuple-element.21, f32[1,320,2560]{2,1,0:T(8,128)} %param.17, f32[]{:T(128)} %bitcast.10, f32[]{:T(128)} %bitcast.8, f32[1,320,2560]{2,1,0:T(8,128)} %param.16, f32[320,2560]{1,0:T(8,128)} %get-tuple-element.22, ...), kind=kLoop, calls=%fused_computation.25 | loop fusion | flops 13926400 | bytes 26214408 | tf_op jit(solution)/shard_map/broadcast_in_dim | solution.py:86
  (2 shorter events, 0.0 us)
Async XLA Ops:
  7.2 170.3 %all-gather.3.cloned.1.call-start = ((), (), s32[]{:S(2)}) async-start(), calls=%async_computation.2 | async-start | bytes 22282240 | tf_op jit(solution)/shard_map/all_gather | solution.py:58
  12.3 61.4 %all-to-all-start = ((bf16[256,16,320]{0,2,1:T(8,128)(2,1)}), bf16[256,16,320]{0,2,1:T(8,128)(2,1)S(1)}, u32[]{:S(2)}, u32[]{:S(2)}) async-start(bf16[256,16,320]{0,2,1:T(8,128)(2,1)} %bitcast.3), calls=%async_computation | async-start | bytes 5242880 | tf_op jit(solution)/shard_map/all_to_all | solution.py:61
  22.2 58.8 %copy-start.1 = (bf16[320]{0:T(512)(128)(2,1)S(1)}, bf16[320]{0:T(512)(128)(2,1)}, u32[]{:S(2)}) copy-start(bf16[320]{0:T(512)(128)(2,1)} %param.14) | copy-start | bytes 1924
  73.7 66.3 %all-to-all-start.1 = ((bf16[256,16,320]{0,2,1:T(8,128)(2,1)}), bf16[256,16,320]{0,2,1:T(8,128)(2,1)}, u32[]{:S(2)}, u32[]{:S(2)}) async-start(bf16[256,16,320]{0,2,1:T(8,128)(2,1)} %bitcast.6), calls=%async_computation.1 | async-start | bytes 5242880 | tf_op jit(solution)/shard_map/all_to_all | solution.py:62
  142.3 35.3 %copy-start = (f32[1,320,2560]{2,1,0:T(8,128)S(1)}, f32[1,320,2560]{2,1,0:T(8,128)}, u32[]{:S(2)}) copy-start(f32[1,320,2560]{2,1,0:T(8,128)} %param.15) | copy-start | bytes 9830404
  276.4 69.4 %collective-permute-start = (f32[320,2560]{1,0:T(8,128)}, f32[320,2560]{1,0:T(8,128)}, u32[]{:S(2)}, u32[]{:S(2)}) collective-permute-start(f32[320,2560]{1,0:T(8,128)} %param), channel_id=1, source_target_pairs={{0,16},{16,0},{32,48},{48,32},{64,80},{80,64},{96,112},{112,96},{1... | collective-permute-start | bytes 9830408 | tf_op jit(solution)/shard_map/cond/branch_0_fun/ppermute | solution.py:18
Sparse Core Ops, SparseCore 0:
  9.7 167.7 all-gather.2
where the time goes:
time: 362 us; the launch traced here: 361 us
  waiting for transfers between devices  207 us (57%)
  blocking collectives  55.2 us (15%)
  matrix products  43.6 us (12%)
  between operations  14.8 us (4%)
  local copies, waits for them, and re-layouts  14.7 us (4%)
  starting transfers between devices  14.1 us (4%)
  other arithmetic  11.6 us (3%)
    ppermute x1, waiting for transfers between devices, partner(): return lax.ppermute(value, axis, pairs)  67.5 us
    all_to_all x1, waiting for transfers between devices, per_device(): lax.all_to_all(cotangent[0], 'fsdp', split_axis=1, concat_axis=0, tiled=T...  55.3 us
    psum x1, blocking collectives, per_device(): lax.psum(jnp.sum(pre_norm * scaled, axis=1).astype(jnp.bfloat16), 'fsdp')  55.2 us
    all_to_all x1, waiting for transfers between devices, per_device(): lax.all_to_all(residual[0], 'fsdp', split_axis=1, concat_axis=0, tiled=True)  51.5 us
    all_gather x1, waiting for transfers between devices, per_device(): full_attn = lax.all_gather(local_attn, 'fsdp', axis=0, tiled=True)  32.3 us
    dot_general x1, matrix products, per_device(): lax.dot_general(full_attn, w_half, contract_feat, preferred_element_type=...  24.1 us
    dot_general x1, matrix products, per_device(): lax.dot_general(grad_pre, full_attn, contract_rows, preferred_element_typ...  19.5 us
    unnamed x6, local copies, waits for them, and re-layouts  8.77 us
  transfers between devices with their start and end apart: 4, of which 4 were waited for; matrix products, arithmetic and copies ran while one was open for 5% of the time, Pallas kernels for 0%

commit v1 on v0

--- a/solution.py
+++ b/solution.py
@@ -55,7 +55,9 @@
     w_half = params_local.astype(jnp.bfloat16)
     contract_feat = (((1,), (1,)), ((), ()))
     contract_rows = (((0,), (0,)), ((), ()))
-    full_attn = lax.all_gather(local_attn, "fsdp", axis=0, tiled=True)
+    full_attn = jnp.concatenate(
+        lax.all_to_all(jnp.stack([local_attn] * lax.axis_size("fsdp")), "fsdp", 0, 0), axis=0
+    )
     pre_cols = lax.dot_general(full_attn, w_half, contract_feat, preferred_element_type=jnp.float32)
     resid_cols, cotan_cols = (
         lax.all_to_all(residual[0], "fsdp", split_axis=1, concat_axis=0, tiled=True),

time: 362 us -> 552 us (1.52)
  waiting for transfers between devices: 207 us -> 371 us
  blocking collectives: 55.2 us -> 90.4 us
  between operations: 14.8 us -> 1.47 us
  local copies, waits for them, and re-layouts: 14.7 us -> 20.6 us
    all_to_all x1, waiting for transfers between devices: 51.5 us -> 271 us  [per_device(): lax.all_to_all(jnp.stack([local_attn] * lax.axis_size('fsdp')), 'fsdp', 0...]
    all_to_all x0 -> x1, blocking collectives: none -> 37.5 us  [per_device(): lax.all_to_all(residual[0], 'fsdp', split_axis=1, concat_axis=0, tiled=True)]
    all_gather x1 -> x0, waiting for transfers between devices: 32.3 us -> none  [per_device(): full_attn = lax.all_gather(local_attn, 'fsdp', axis=0, tiled=True)]
    all_to_all x1, waiting for transfers between devices: 55.3 us -> 32.3 us  [per_device(): lax.all_to_all(cotangent[0], 'fsdp', split_axis=1, concat_axis=0, tiled=T...]
    another operation x0 -> x1, local copies, waits for them, and re-layouts: none -> 7.36 us  [per_device(): jnp.stack([local_attn] * lax.axis_size('fsdp'))]
  transfers between devices with their start and end apart: 4 -> 3, of which waited for: 4 -> 3; matrix products, arithmetic and copies ran while one was open for 5% -> 2% of each run, Pallas kernels for 0% -> 0%
where the time goes in v1:
time: 552 us; the launch traced here: 551 us
  waiting for transfers between devices  371 us (67%)
  blocking collectives  90.4 us (16%)
  matrix products  43.7 us (8%)
  local copies, waits for them, and re-layouts  20.6 us (4%)
  starting transfers between devices  13 us (2%)
  other arithmetic  11.6 us (2%)
    all_to_all x1, waiting for transfers between devices, per_device(): lax.all_to_all(jnp.stack([local_attn] * lax.axis_size('fsdp')), 'fsdp', 0...  271 us
    ppermute x1, waiting for transfers between devices, partner(): return lax.ppermute(value, axis, pairs)  67.5 us
    psum x1, blocking collectives, per_device(): lax.psum(jnp.sum(pre_norm * scaled, axis=1).astype(jnp.bfloat16), 'fsdp')  52.9 us
    all_to_all x1, blocking collectives, per_device(): lax.all_to_all(residual[0], 'fsdp', split_axis=1, concat_axis=0, tiled=True)  37.5 us
    all_to_all x1, waiting for transfers between devices, per_device(): lax.all_to_all(cotangent[0], 'fsdp', split_axis=1, concat_axis=0, tiled=T...  32.3 us
    dot_general x1, matrix products, per_device(): lax.dot_general(full_attn, w_half, contract_feat, preferred_element_type=...  24.2 us
    dot_general x1, matrix products, per_device(): lax.dot_general(grad_pre, full_attn, contract_rows, preferred_element_typ...  19.5 us
  transfers between devices with their start and end apart: 3, of which 3 were waited for; matrix products, arithmetic and copies ran while one was open for 2% of the time, Pallas kernels for 0%

profile of v1, /device:TPU:0, one launch (start us, length us, event | category | flops | bytes accessed | tf_op | source)
XLA Modules:
  0.0 551.4 jit_solution(15665954040739767595)
XLA Ops:
  0.6 4.4 copy.15
  5.0 5.6 %all-to-all-start.2 = ((bf16[256,16,320]{0,2,1:T(8,128)(2,1)}), bf16[256,16,320]{0,2,1:T(8,128)(2,1)}, u32[]{:S(2)}, u32[]{:S(2)}) async-start(bf16[256,16,320]{0,2,1:T(8,128)(2,1)} %bitcast.8), calls=%async_computation.2 | async-start | bytes 5242880 | tf_op jit(solution)/shard_map/all_to_all | solution.py:64
  10.6 3.0 copy.13
  13.6 32.3 %all-to-all-done.2 = bf16[256,16,320]{0,2,1:T(8,128)(2,1)} async-done(((bf16[256,16,320]{0,2,1:T(8,128)(2,1)}), bf16[256,16,320]{0,2,1:T(8,128)(2,1)}, u32[]{:S(2)}, u32[]{:S(2)}) %all-to-all-start.2) | async-done | bytes 2621472 | tf_op jit(solution)/shard_map/all_to_all | solution.py:64
  45.8 0.0 copy-start.2
  45.8 37.5 %all_to_all.31 = bf16[256,16,320]{0,2,1:T(8,128)(2,1)} all-to-all(bf16[256,16,320]{0,2,1:T(8,128)(2,1)S(1)} %bitcast.64), channel_id=1, replica_groups=mesh['rep'=8,'fsdp'=16] {'fsdp'}, dimensions={1} | all-to-all | bytes 5242880 | tf_op jit(solution)/shard_map/all_to_all | solution.py:63
  83.3 0.0 copy-done.2
  83.3 7.4 %stack.3 = bf16[16,256,2560]{2,1,0:T(8,128)(2,1)} broadcast(bf16[256,2560]{1,0:T(8,128)(2,1)S(1)} %bitcast.68), dimensions={1,2} | broadcast | bytes 22282240 | tf_op jit(solution)/shard_map/stack | solution.py:59
  90.7 0.0 copy-start.3
  90.7 5.5 all-to-all-start.1
  96.8 0.0 copy-done.3
  96.9 2.3 convert_bitcast_fusion
  99.2 0.0 copy-start
  99.3 3.0 copy.18
  102.2 0.0 copy-done
  102.2 0.6 convert_bitcast_fusion.1
  102.8 0.0 copy-start.1
  102.8 2.9 copy.17
  105.7 271.0 %all-to-all-done.1 = bf16[16,256,2560]{2,1,0:T(8,128)(2,1)} async-done(((bf16[16,256,2560]{2,1,0:T(8,128)(2,1)}), bf16[16,256,2560]{2,1,0:T(8,128)(2,1)}, u32[]{:S(2)}, u32[]{:S(2)}) %all-to-all-start.1) | async-done | bytes 20971552 | tf_op jit(solution)/shard_map/all_to_all | solution.py:59
  376.7 0.0 copy-done.1
  376.7 24.2 %multiply_reduce_fusion.1 = (bf16[4096]{0:T(1024)(128)(2,1)S(1)}, bf16[4096]{0:T(1024)(128)(2,1)S(1)}, f32[4096,320]{0,1:T(8,128)}) fusion(f32[4096,320]{0,1:T(8,128)} %bitcast.65, f32[320]{0:T(512)S(1)} %convert_element_type.53, f32[4096,320]{0,1:T(8,128)} %bitcast.67, bf16[4096,2560]{1,0:T(8,128)(2,1)} %bitcast.6, f32[1,320,2560]{2,1,0:T(8,128)S(1)} %copy-done.1), kind=kOutput, calls=%fused_computation.5 | convolution fusion | flops 6719561728 | bytes 39994624 | tf_op jit(solution)/shard_map/dot_general | solution.py:61
  400.8 52.9 %all-reduce = (bf16[4096]{0:T(1024)(128)(2,1)S(1)}, bf16[4096]{0:T(1024)(128)(2,1)S(1)}) all-reduce(bf16[4096]{0:T(1024)(128)(2,1)S(1)} %get-tuple-element.11, bf16[4096]{0:T(1024)(128)(2,1)S(1)} %get-tuple-element.10), channel_id=1, replica_groups=mesh['rep'=8,'fsdp'=16] {'fsdp'}, use_global_device_ids=true, to_apply=%region_3.0 | all-reduce | flops 8192 | bytes 32768 | tf_op jit(solution)/shard_map/psum | solution.py:72
  453.8 19.5 %bitcast_add_fusion.1 = (f32[320,2560]{1,0:T(8,128)}, f32[320,2560]{1,0:T(8,128)}) fusion(f32[1,320,2560]{2,1,0:T(8,128)S(1)} %copy-done.1, f32[]{:T(128)} %bitcast.12, f32[1,320,2560]{2,1,0:T(8,128)} %param.17, f32[]{:T(128)} %bitcast.10, f32[1,320,2560]{2,1,0:T(8,128)} %param.16, bf16[4096,2560]{1,0:T(8,128)(2,1)} %bitcast.6, ...), kind=kOutput, calls=%fused_computation.10 | convolution fusion | flops 6729728000 | bytes 47875336 | tf_op jit(solution)/shard_map/dot_general | solution.py:77
  473.3 69.4 %conditional.1 = (f32[320,2560]{1,0:T(8,128)}) conditional(s32[]{:T(128)} %clamp.3, f32[320,2560]{1,0:T(8,128)} %get-tuple-element.20, f32[320,2560]{1,0:T(8,128)} %get-tuple-element.20, f32[320,2560]{1,0:T(8,128)} %get-tuple-element.20), branch_computations={%region_4.5_spmd, %region_5.6_spmd, %region_6.7_spmd} | conditional | bytes 13107248 | solution.py:46
  473.3 1.9 collective-permute-start
  475.2 67.5 %collective-permute-done = f32[320,2560]{1,0:T(8,128)} collective-permute-done((f32[320,2560]{1,0:T(8,128)}, f32[320,2560]{1,0:T(8,128)}, u32[]{:S(2)}, u32[]{:S(2)}) %collective-permute-start) | collective-permute-done | bytes 3276832 | tf_op jit(solution)/shard_map/cond/branch_0_fun/ppermute | solution.py:18
  542.6 8.7 %fusion.12 = (f32[1,320,2560]{2,1,0:T(8,128)}, f32[1,320,2560]{2,1,0:T(8,128)}, f32[1,320,2560]{2,1,0:T(8,128)}) fusion(f32[320,2560]{1,0:T(8,128)} %get-tuple-element.21, f32[1,320,2560]{2,1,0:T(8,128)} %param.17, f32[]{:T(128)} %bitcast.12, f32[]{:T(128)} %bitcast.10, f32[1,320,2560]{2,1,0:T(8,128)} %param.16, f32[320,2560]{1,0:T(8,128)} %get-tuple-element.22, ...), kind=kLoop, calls=%fused_computation.23 | loop fusion | flops 13926400 | bytes 26214408 | tf_op jit(solution)/shard_map/broadcast_in_dim | solution.py:88
  (2 shorter events, 0.0 us)
Async XLA Ops:
  5.0 40.8 %all-to-all-start.2 = ((bf16[256,16,320]{0,2,1:T(8,128)(2,1)}), bf16[256,16,320]{0,2,1:T(8,128)(2,1)}, u32[]{:S(2)}, u32[]{:S(2)}) async-start(bf16[256,16,320]{0,2,1:T(8,128)(2,1)} %bitcast.8), calls=%async_computation.2 | async-start | bytes 5242880 | tf_op jit(solution)/shard_map/all_to_all | solution.py:64
  45.8 37.5 %copy-start.2 = (bf16[1,256,2560]{2,1,0:T(8,128)(2,1)S(1)}, bf16[1,256,2560]{2,1,0:T(8,128)(2,1)}, u32[]{:S(2)}) copy-start(bf16[1,256,2560]{2,1,0:T(8,128)(2,1)} %param.11) | copy-start | bytes 3932164
  90.7 6.1 %copy-start.3 = (bf16[320]{0:T(512)(128)(2,1)S(1)}, bf16[320]{0:T(512)(128)(2,1)}, u32[]{:S(2)}) copy-start(bf16[320]{0:T(512)(128)(2,1)} %param.14) | copy-start | bytes 1924
  90.7 286.0 %all-to-all-start.1 = ((bf16[16,256,2560]{2,1,0:T(8,128)(2,1)}), bf16[16,256,2560]{2,1,0:T(8,128)(2,1)}, u32[]{:S(2)}, u32[]{:S(2)}) async-start(bf16[16,256,2560]{2,1,0:T(8,128)(2,1)} %stack.3), calls=%async_computation.1 | async-start | bytes 41943040 | tf_op jit(solution)/shard_map/all_to_all | solution.py:59
  99.2 3.0 copy-start
  102.8 273.9 %copy-start.1 = (f32[1,320,2560]{2,1,0:T(8,128)S(1)}, f32[1,320,2560]{2,1,0:T(8,128)}, u32[]{:S(2)}) copy-start(f32[1,320,2560]{2,1,0:T(8,128)} %param.15) | copy-start | bytes 9830404
  473.3 69.4 %collective-permute-start = (f32[320,2560]{1,0:T(8,128)}, f32[320,2560]{1,0:T(8,128)}, u32[]{:S(2)}, u32[]{:S(2)}) collective-permute-start(f32[320,2560]{1,0:T(8,128)} %param), channel_id=1, source_target_pairs={{0,16},{16,0},{32,48},{48,32},{64,80},{80,64},{96,112},{112,96},{1... | collective-permute-start | bytes 9830408 | tf_op jit(solution)/shard_map/cond/branch_0_fun/ppermute | solution.py:18
